TPU v7x, 512 devices: a whole 4x8x8 slice. The times are simulated.
512 devices in a mesh: dp: 32 (over y_hi, z), inblk: 4 (over x), outcol: 4 (over y_lo, core).
Axes of the slice: x: 4, y: 8 (y_hi: 4, y_lo: 2; y = y_hi * 2 + y_lo), z: 8, core: 2. Of those that a mesh axis runs over, the one named last changes fastest.
Arguments:
- activations: bfloat16 [4096, 8192], P('dp', ('inblk', 'outcol')), may hold values from -1.5 to 1.5
- cotangent: bfloat16 [4096, 1024], P('dp', 'outcol'), may hold values from -6 to 6
- base_weight: bfloat16 [8192, 1024], P('inblk', 'outcol'), may hold values from -0.09375 to 0.09375
- skew_param: float32 [32, 256, 256], P(('inblk', 'outcol'), 'dp'), may hold values from -0.3125 to 0.3125
Outputs:
- grad_acts: bfloat16 [4096, 8192], P('dp', ('inblk', 'outcol'))
- grad_skew: float32 [32, 256, 256], P(('inblk', 'outcol'), 'dp')
All inputs are finite; a program needn't handle non-finite values.
Results may differ from a plain program's by a relative error of at most 0.0058.
Values may be sent and summed in bfloat16 or wider, within the bound.
No kernel may reach another device: no remote copies, remote signals or barrier semaphores. Data moves between devices by JAX's collectives and lax.ppermute only.
A program may use at most 64 MiB of HBM per device.

v0:
```python
import jax
import jax.numpy as jnp
from jax import lax
from jax.sharding import PartitionSpec as P


def high_product(left, right):
    return jnp.matmul(left, right, precision=lax.Precision.HIGHEST)


def power_list(skew_input):
    skew_mat = skew_input - jnp.swapaxes(skew_input, -1, -2)
    powers = [skew_mat]
    for degree in range(5):
        powers.append(high_product(powers[-1], skew_mat))
    return powers


def rotation_of(powers):
    block_width = powers[0].shape[-1]
    identity_mat = jnp.eye(block_width, dtype=jnp.float32)
    series = powers[0] + powers[1] + powers[2] + powers[3] + powers[4]
    return identity_mat + 2.0 * series + powers[5]


def chain_rule(grad_rot, powers):
    negated = [powers[degree] * (-1.0) ** (degree + 1) for degree in range(5)]
    partial_value = grad_rot
    running = 2.0 * grad_rot
    for degree in range(2, 7):
        partial_value = high_product(negated[0], partial_value) + high_product(
            grad_rot, negated[degree - 2]
        )
        weight_factor = 2.0 if degree < 6 else 1.0
        running = running + weight_factor * partial_value
    return running - jnp.swapaxes(running, -1, -2)


def body(activations, cotangent, base_weight, skew_param):
    full_skew = lax.all_gather(skew_param, "dp", axis=1, tiled=True)
    powers = power_list(full_skew)
    rotation = rotation_of(powers).astype(jnp.bfloat16)
    token_count = activations.shape[0]
    own_width = activations.shape[1]
    block_count = full_skew.shape[0]
    block_width = full_skew.shape[2]
    features = lax.psum_scatter(
        lax.dot_general(
            base_weight, cotangent, (((1,), (1,)), ((), ())), preferred_element_type=jnp.float32
        ),
        "outcol",
        scatter_dimension=0,
        tiled=True,
    )
    features = features.astype(jnp.bfloat16).reshape(block_count, block_width, token_count)
    grad_t = jnp.einsum(
        "bij,bjt->bit", rotation, features, preferred_element_type=jnp.float32
    ).astype(jnp.bfloat16)
    grad_acts = jnp.transpose(grad_t.reshape(own_width, token_count))
    grad_rot = jnp.einsum(
        "tbi,bjt->bij",
        activations.reshape(token_count, block_count, block_width),
        features,
        preferred_element_type=jnp.float32,
    )
    summed = lax.psum(grad_rot, "dp")
    grad_full = chain_rule(summed, powers)
    share_rows = block_width // lax.axis_size("dp")
    grad_skew = lax.dynamic_slice_in_dim(
        grad_full, lax.axis_index("dp") * share_rows, share_rows, 1
    )
    return (grad_acts, grad_skew)


def solution(mesh):
    return jax.shard_map(
        body,
        mesh=mesh,
        in_specs=(
            P("dp", ("inblk", "outcol")),
            P("dp", "outcol"),
            P("inblk", "outcol"),
            P(("inblk", "outcol"), "dp", None),
        ),
        out_specs=(P("dp", ("inblk", "outcol")), P(("inblk", "outcol"), "dp", None)),
        check_vma=False,
    )
```

profile of v0, /device:TPU:2, one launch (start us, length us, event | category | flops | bytes accessed | tf_op | source)
XLA Modules:
  0.0 434.7 jit_solution(13331793487568071938)
XLA Ops:
  7.2 0.0 copy-start
  7.2 0.0 reduce-scatter.2.cloned.1.call-start
  7.2 1.2 copy-done
  8.4 2.2 fusion.38
  10.6 0.0 copy-start.4
  10.6 0.0 reduce-scatter.2.cloned.1.call-update
  10.7 0.0 all-reduce.2.cloned.1.call-start
  10.7 0.6 copy-done.4
  11.4 92.4 %all_gather.3 = f32[2,256,256]{2,0,1:T(2,128)S(1)} all-gather(f32[2,8,256]{2,0,1:T(2,128)S(1)} %copy.12), channel_id=1, replica_groups=mesh['dp'=32,'inblk'=4,'outcol'=4] {'dp'}, dimensions={1}, use_global_device_ids=true | all-gather | bytes 540672 | tf_op jit(solution)/shard_map/all_gather | solution.py:40
  103.8 0.2 copy.13
  104.0 0.1 bitcast_subtract_fusion
  104.1 0.7 fusion.34
  104.7 0.7 fusion.35
  105.4 0.7 fusion.36
  106.1 1.5 fusion.37
  107.5 0.0 reduce-scatter.2.cloned.1.call-done
  107.5 0.0 copy-start.3
  107.5 1.0 convert_element_type.18
  108.5 0.0 copy-done.3
  108.5 1.1 convolution_bitcast_fusion
  109.6 0.0 all-reduce.2.cloned.1.call-update
  109.6 1.9 fusion.1
  111.6 0.2 convolution_convert_fusion
  111.8 0.8 copy.15
  112.5 306.2 %all-reduce.2.cloned.1.call-done = f32[2,256,256]{2,1,0:T(8,128)} async-done(((f32[2,256,256]{2,1,0:T(8,128)}), f32[2,256,256]{2,1,0:T(8,128)}) %all-reduce.2.cloned.1.call-update) | async-done | bytes 524304 | tf_op jit(solution)/shard_map/psum | solution.py:66
  418.7 0.0 copy-start.1
  418.7 1.8 fusion.13
  420.5 0.0 copy-done.1
  420.5 0.7 convolution_add_fusion.4
  421.2 0.7 fusion.10
  421.9 0.7 convolution_add_fusion.3
  422.6 0.7 fusion.8
  423.2 0.7 convolution_add_fusion.2
  423.9 0.7 fusion.6
  424.6 0.7 convolution_add_fusion.1
  425.2 0.0 copy-start.2
  425.3 0.7 fusion.4
  425.9 0.4 copy-done.2
  426.3 0.7 fusion
  427.0 0.2 copy.18
  427.2 0.6 dynamic-slice_subtract_fusion
  (2 shorter events, 0.0 us)
Async XLA Ops:
  7.2 1.2 copy-start
  7.2 100.3 %reduce-scatter.2.cloned.1.call-start = ((), (), s32[]{:S(2)}) async-start(), calls=%async_computation.1 | async-start | bytes 1310720 | tf_op jit(solution)/shard_map/reduce_scatter | solution.py:47
  10.6 0.7 copy-start.4
  10.7 408.1 %all-reduce.2.cloned.1.call-start = ((), (), s32[]{:S(2)}) async-start(), calls=%async_computation.2 | async-start | bytes 1048576 | tf_op jit(solution)/shard_map/psum | solution.py:66
  107.5 1.0 copy-start.3
  418.7 1.8 copy-start.1
  425.2 1.0 copy-start.2
Sparse Core Ops, SparseCore 0:
  10.9 31.1 reduce-scatter.1
  109.8 308.9 all-reduce.1
where the time goes:
time: 435 us
  waiting for transfers between devices  306 us (70%)
  blocking collectives  92.4 us (21%)
  matrix products  16.7 us (4%)
  between operations  14.2 us (3%)
    psum x1, waiting for transfers between devices, body(): summed = lax.psum(grad_rot, 'dp')  306 us
    all_gather x1, blocking collectives, body(): full_skew = lax.all_gather(skew_param, 'dp', axis=1, tiled=True)  92.4 us
    dot_general x15, matrix products, high_product(): return jnp.matmul(left, right, precision=lax.Precision.HIGHEST)  13.2 us
  transfers between devices with their start and end apart: 2, of which 1 were waited for; matrix products, arithmetic and copies ran while one was open for 2% of the time, Pallas kernels for 0%

commit v1 on v0

--- a/solution.py
+++ b/solution.py
@@ -63,7 +63,8 @@
         features,
         preferred_element_type=jnp.float32,
     )
-    summed = lax.psum(grad_rot, "dp")
+    terms = lax.all_gather(grad_rot, "dp", axis=0, tiled=False)
+    summed = terms.sum(axis=0)
     grad_full = chain_rule(summed, powers)
     share_rows = block_width // lax.axis_size("dp")
     grad_skew = lax.dynamic_slice_in_dim(

time: 435 us -> 290 us (0.67)
  waiting for transfers between devices: 306 us -> 154 us
  other arithmetic: 1.71 us -> 8.09 us
    psum x1 -> x0, waiting for transfers between devices: 306 us -> none  [body(): summed = lax.psum(grad_rot, 'dp')]
    all_gather x0 -> x1, waiting for transfers between devices: none -> 124 us  [body(): terms = lax.all_gather(grad_rot, 'dp', axis=0, tiled=False)]
    reduce_scatter x1, waiting for transfers between devices: 0.01 us -> 30.3 us  [body(): lax.psum_scatter(lax.dot_general(base_weight, cotangent, (((1,), (1,)), (...]
    unnamed x0 -> x1, other arithmetic: none -> 6.89 us
  transfers between devices with their start and end apart: 2 -> 2, of which waited for: 1 -> 2; matrix products, arithmetic and copies ran while one was open for 2% -> 2% of each run, Pallas kernels for 0% -> 0%
where the time goes in v1:
time: 290 us; the launch traced here: 289 us
  waiting for transfers between devices  154 us (53%)
  blocking collectives  92.3 us (32%)
  matrix products  15.7 us (5%)
  between operations  14.3 us (5%)
  other arithmetic  8.09 us (3%)
  local copies, waits for them, and re-layouts  4.75 us (2%)
    all_gather x1, waiting for transfers between devices, body(): terms = lax.all_gather(grad_rot, 'dp', axis=0, tiled=False)  124 us
    all_gather x1, blocking collectives, body(): full_skew = lax.all_gather(skew_param, 'dp', axis=1, tiled=True)  92.3 us
    reduce_scatter x1, waiting for transfers between devices, body(): lax.psum_scatter(lax.dot_general(base_weight, cotangent, (((1,), (1,)), (...  30.3 us
    dot_general x15, matrix products, high_product(): return jnp.matmul(left, right, precision=lax.Precision.HIGHEST)  12.2 us
    unnamed x1, other arithmetic  6.89 us
  transfers between devices with their start and end apart: 2, of which 2 were waited for; matrix products, arithmetic and copies ran while one was open for 2% of the time, Pallas kernels for 0%

profile of v1, /device:TPU:2, one launch (start us, length us, event | category | flops | bytes accessed | tf_op | source)
XLA Modules:
  0.0 289.2 jit_solution(7865287874692615054)
XLA Ops:
  7.2 0.0 copy-start
  7.2 0.0 reduce-scatter.2.cloned.1.call-start
  7.2 1.2 copy-done
  8.4 2.2 fusion.38
  10.6 0.0 reduce-scatter.2.cloned.1.call-update
  10.7 0.0 all-gather.3.cloned.1.call-start
  10.7 30.3 %reduce-scatter.2.cloned.1.call-done = f32[512,128]{1,0:T(8,128)} async-done(((f32[2048,128]{1,0:T(8,128)}), f32[512,128]{1,0:T(8,128)}) %reduce-scatter.2.cloned.1.call-update) | async-done | bytes 262160 | tf_op jit(solution)/shard_map/reduce_scatter | solution.py:47
  41.0 1.0 convert_element_type.18
  42.0 1.1 convolution_bitcast_fusion
  43.1 1.0 copy.17
  44.1 0.0 all-gather.3.cloned.1.call-update
  44.1 0.7 copy.12
  44.9 92.3 %all_gather.9 = f32[2,256,256]{2,0,1:T(2,128)S(1)} all-gather(f32[2,8,256]{2,0,1:T(2,128)S(1)} %copy.12), channel_id=1, replica_groups=mesh['dp'=32,'inblk'=4,'outcol'=4] {'dp'}, dimensions={1}, use_global_device_ids=true | all-gather | bytes 540672 | tf_op jit(solution)/shard_map/all_gather | solution.py:40
  137.2 0.2 copy.13
  137.4 0.1 bitcast_subtract_fusion
  137.5 0.6 fusion.34
  138.2 0.0 copy-start.1
  138.2 0.7 fusion.35
  138.8 0.7 fusion.36
  139.5 0.7 fusion.37
  140.1 0.0 copy-done.1
  140.2 0.0 copy-start.2
  140.2 0.8 fusion.1
  141.0 0.0 copy-done.2
  141.0 0.2 convolution_convert_fusion
  141.2 0.8 copy.15
  142.0 123.6 %all-gather.3.cloned.1.call-done = f32[64,256,256]{2,1,0:T(8,128)} async-done(((f32[2,256,256]{2,1,0:T(8,128)}), f32[64,256,256]{2,1,0:T(8,128)}) %all-gather.3.cloned.1.call-update) | async-done | bytes 16777232 | tf_op jit(solution)/shard_map/all_gather | solution.py:66
  265.6 6.9 %reduce_sum.9 = f32[2,256,256]{2,1,0:T(8,128)S(1)} reduce(f32[32,2,256,256]{3,2,1,0:T(8,128)} %bitcast.40, f32[]{:T(128)} %constant.3.clone.1), dimensions={0}, to_apply=%region_1.0 | reduce | flops 4063232 | bytes 17301508
  272.5 0.7 fusion.13
  273.2 0.7 convolution_add_fusion.4
  273.9 0.7 fusion.10
  274.5 1.7 convolution_add_fusion.3
  276.2 0.7 fusion.8
  276.9 0.7 convolution_add_fusion.2
  277.6 0.7 fusion.6
  278.3 0.7 convolution_add_fusion.1
  278.9 0.7 fusion.4
  279.6 1.8 fusion
  281.4 0.1 copy.35
  281.5 0.1 dynamic-slice_subtract_fusion
  281.7 0.7 copy.27
  (2 shorter events, 0.0 us)
Async XLA Ops:
  7.2 1.2 copy-start
  7.2 33.8 %reduce-scatter.2.cloned.1.call-start = ((), (), s32[]{:S(2)}) async-start(), calls=%async_computation.1 | async-start | bytes 1310720 | tf_op jit(solution)/shard_map/reduce_scatter | solution.py:47
  10.7 255.0 %all-gather.3.cloned.1.call-start = ((), (), s32[]{:S(2)}) async-start(), calls=%async_computation.2 | async-start | bytes 17301504 | tf_op jit(solution)/shard_map/all_gather | solution.py:66
  138.2 2.0 copy-start.1
  140.2 0.8 copy-start.2
Sparse Core Ops, SparseCore 0:
  10.9 30.1 reduce-scatter.1
  44.7 220.8 all-gather.2

commit v2 on v0

--- a/solution.py
+++ b/solution.py
@@ -37,7 +37,11 @@
 
 
 def body(activations, cotangent, base_weight, skew_param):
-    full_skew = lax.all_gather(skew_param, "dp", axis=1, tiled=True)
+    _fit_tracks = lambda q_in, mesh_dim: jnp.concatenate(
+        jax.lax.all_to_all(jnp.stack([q_in] * jax.lax.axis_size(mesh_dim), axis=0), mesh_dim, 0, 0),
+        axis=1,
+    )
+    full_skew = _fit_tracks(skew_param, "dp")
     powers = power_list(full_skew)
     rotation = rotation_of(powers).astype(jnp.bfloat16)
     token_count = activations.shape[0]

time: 435 us -> 392 us (0.901)
  blocking collectives: 92.4 us -> 0 us
  waiting for transfers between devices: 306 us -> 340 us
  starting transfers between devices: 0.08 us -> 16.2 us
    all_gather x1 -> x0, blocking collectives: 92.4 us -> none  [body(): full_skew = lax.all_gather(skew_param, 'dp', axis=1, tiled=True)]
    all_to_all x0 -> x1, waiting for transfers between devices: none -> 17.2 us  [body(): jax.lax.all_to_all(jnp.stack([q_in] * jax.lax.axis_size(mesh_dim), axis=0...]
    all_to_all x0 -> x1, starting transfers between devices: none -> 16.1 us  [body(): jax.lax.all_to_all(jnp.stack([q_in] * jax.lax.axis_size(mesh_dim), axis=0...]
    psum x1, waiting for transfers between devices: 306 us -> 316 us  [body(): summed = lax.psum(grad_rot, 'dp')]
    reduce_scatter x1, waiting for transfers between devices: 0.01 us -> 7.47 us  [body(): lax.psum_scatter(lax.dot_general(base_weight, cotangent, (((1,), (1,)), (...]
  transfers between devices with their start and end apart: 2 -> 3, of which waited for: 1 -> 3; matrix products, arithmetic and copies ran while one was open for 2% -> 2% of each run, Pallas kernels for 0% -> 0%
where the time goes in v2:
time: 392 us; the launch traced here: 391 us
  waiting for transfers between devices  340 us (87%)
  starting transfers between devices  16.2 us (4%)
  matrix products  15.9 us (4%)
  between operations  14.3 us (4%)
    psum x1, waiting for transfers between devices, body(): summed = lax.psum(grad_rot, 'dp')  316 us
    all_to_all x1, waiting for transfers between devices, body(): jax.lax.all_to_all(jnp.stack([q_in] * jax.lax.axis_size(mesh_dim), axis=0...  17.2 us
    all_to_all x1, starting transfers between devices, body(): jax.lax.all_to_all(jnp.stack([q_in] * jax.lax.axis_size(mesh_dim), axis=0...  16.1 us
    dot_general x15, matrix products, high_product(): return jnp.matmul(left, right, precision=lax.Precision.HIGHEST)  13.2 us
  transfers between devices with their start and end apart: 3, of which 3 were waited for; matrix products, arithmetic and copies ran while one was open for 2% of the time, Pallas kernels for 0%

profile of v2, /device:TPU:2, one launch (start us, length us, event | category | flops | bytes accessed | tf_op | source)
XLA Modules:
  0.0 391.5 jit_solution(10305173627145851325)
XLA Ops:
  7.2 0.0 copy-start
  7.2 1.7 stack.2
  8.9 0.0 copy-start.4
  8.9 16.1 %all-to-all-start = ((f32[32,2,8,256]{3,2,1,0:T(8,128)}), f32[32,2,8,256]{3,2,1,0:T(8,128)S(1)}, u32[]{:S(2)}, u32[]{:S(2)}) async-start(f32[32,2,8,256]{3,2,1,0:T(8,128)} %stack.2), calls=%async_computation | async-start | bytes 1048576 | tf_op jit(solution)/shard_map/all_to_all | solution.py:41
  25.0 0.0 reduce-scatter.2.cloned.1.call-start
  25.0 0.0 copy-done
  25.0 0.0 copy-done.4
  25.0 1.4 fusion.38
  26.4 0.0 reduce-scatter.2.cloned.1.call-update
  26.5 0.0 all-reduce.2.cloned.1.call-start
  26.5 17.2 %all-to-all-done = f32[32,2,8,256]{3,2,1,0:T(8,128)S(1)} async-done(((f32[32,2,8,256]{3,2,1,0:T(8,128)}), f32[32,2,8,256]{3,2,1,0:T(8,128)S(1)}, u32[]{:S(2)}, u32[]{:S(2)}) %all-to-all-start) | async-done | bytes 524320 | tf_op jit(solution)/shard_map/all_to_all | solution.py:41
  43.8 0.2 copy.18
  44.0 0.1 bitcast_subtract_fusion
  44.1 0.7 fusion.34
  44.7 0.7 fusion.35
  45.4 0.7 fusion.36
  46.1 1.5 fusion.37
  47.5 7.5 %reduce-scatter.2.cloned.1.call-done = f32[512,128]{1,0:T(8,128)} async-done(((f32[2048,128]{1,0:T(8,128)}), f32[512,128]{1,0:T(8,128)}) %reduce-scatter.2.cloned.1.call-update) | async-done | bytes 262160 | tf_op jit(solution)/shard_map/reduce_scatter | solution.py:51
  55.0 0.0 copy-start.3
  55.0 1.0 convert_element_type.18
  56.0 0.0 copy-done.3
  56.0 1.1 convolution_bitcast_fusion
  57.1 0.0 all-reduce.2.cloned.1.call-update
  57.1 1.9 fusion.1
  59.0 0.2 convolution_convert_fusion
  59.3 0.8 copy.19
  60.0 315.5 %all-reduce.2.cloned.1.call-done = f32[2,256,256]{2,1,0:T(8,128)} async-done(((f32[2,256,256]{2,1,0:T(8,128)}), f32[2,256,256]{2,1,0:T(8,128)}) %all-reduce.2.cloned.1.call-update) | async-done | bytes 524304 | tf_op jit(solution)/shard_map/psum | solution.py:70
  375.5 0.0 copy-start.1
  375.5 1.8 fusion.13
  377.3 0.0 copy-done.1
  377.3 0.7 convolution_add_fusion.4
  378.0 0.7 fusion.10
  378.7 0.7 convolution_add_fusion.3
  379.3 0.7 fusion.8
  380.0 0.7 convolution_add_fusion.2
  380.7 0.7 fusion.6
  381.4 0.7 convolution_add_fusion.1
  382.0 0.0 copy-start.2
  382.0 0.7 fusion.4
  382.7 0.4 copy-done.2
  383.1 0.7 fusion
  383.8 0.2 copy.22
  384.0 0.6 dynamic-slice_subtract_fusion
  (2 shorter events, 0.1 us)
Async XLA Ops:
  7.2 17.9 %copy-start = (bf16[2048,256]{1,0:T(8,128)(2,1)S(1)}, bf16[2048,256]{1,0:T(8,128)(2,1)}, u32[]{:S(2)}) copy-start(bf16[2048,256]{1,0:T(8,128)(2,1)} %param.6) | copy-start | bytes 3145732
  8.9 16.2 %copy-start.4 = (bf16[128,256]{1,0:T(8,128)(2,1)S(1)}, bf16[128,256]{1,0:T(8,128)(2,1)}, u32[]{:S(2)}) copy-start(bf16[128,256]{1,0:T(8,128)(2,1)} %param.5) | copy-start | bytes 196612
  8.9 34.9 %all-to-all-start = ((f32[32,2,8,256]{3,2,1,0:T(8,128)}), f32[32,2,8,256]{3,2,1,0:T(8,128)S(1)}, u32[]{:S(2)}, u32[]{:S(2)}) async-start(f32[32,2,8,256]{3,2,1,0:T(8,128)} %stack.2), calls=%async_computation | async-start | bytes 1048576 | tf_op jit(solution)/shard_map/all_to_all | solution.py:41
  25.0 30.0 %reduce-scatter.2.cloned.1.call-start = ((), (), s32[]{:S(2)}) async-start(), calls=%async_computation.2 | async-start | bytes 1310720 | tf_op jit(solution)/shard_map/reduce_scatter | solution.py:51
  26.5 349.1 %all-reduce.2.cloned.1.call-start = ((), (), s32[]{:S(2)}) async-start(), calls=%async_computation.3 | async-start | bytes 1048576 | tf_op jit(solution)/shard_map/psum | solution.py:70
  55.0 1.0 copy-start.3
  375.5 1.8 copy-start.1
  382.0 1.0 copy-start.2
Sparse Core Ops, SparseCore 0:
  28.6 26.3 reduce-scatter.1
  58.2 317.3 all-reduce.1
